TPU v7x, 32 devices: a whole 2x2x4 slice. The times are simulated.
32 devices in a mesh: src: 8 (over y, x, core), tgt: 4 (over z).
Axes of the slice: x: 2, y: 2, z: 4, core: 2. Of those that a mesh axis runs over, the one named last changes fastest.
Arguments:
- src_emb: bfloat16 [64, 131072], P(None, 'src'), may hold values from -3 to 3
- tgt_emb: bfloat16 [64, 65536], P(None, 'tgt'), may hold values from -3 to 3
- src_hidden: bfloat16 [64, 131072], P(None, 'src'), may hold values from -4 to 4
- growth: float32 [131072], P('src'), may hold values from -1 to 1
- tgt_mass: float32 [65536], P('tgt'), may hold values from 0.5 to 2
- pair_code: int32 [8, 4, 512], P('src', 'tgt'), may hold values from 0 to 16383, as said below
- pair_count: int32 [8, 4], P('src', 'tgt'), may hold values from 128 to 512, as said below
- block_batch: int32 [1024], P('src'), may hold values from 0 to 31
Outputs:
- src_potential: float32 [131072], P('src')
- tgt_potential: float32 [65536], P('tgt')
- tgt_grad: float32 [64, 65536], P(None, 'tgt')
- adapter_grad: float32 [32, 64, 64], P(('src', 'tgt'))
Inputs may be any that keep to these rules, and one draw needn't show every extreme that they name: `pair_code`: the codes of one device are distinct; among the first 128 entries of each device's list every one of its 128 source blocks and every one of its 128 target blocks appears. `pair_count`: in every draw some device has all 512 entries live.
All inputs are finite; a program needn't handle non-finite values.
Results may differ from a plain program's by a relative error of at most 0.0003.
Values sent between devices are 32-bit elements; how exact they have to be, the bound alone decides.
A program may use at most 192 MiB of HBM per device.

v0:
```python
import math
import jax
import jax.numpy as jnp
from jax import lax
from jax.sharding import PartitionSpec as P

BLK = 128
ENC_DEV = 1
ITERS = 2
entropy_scale = 0.5
update_power = 0.4
highest = lax.Precision.HIGHEST


def rescale(scaling, masses, totals):
    return jnp.sqrt(scaling) * jnp.power(masses / totals, update_power)


def pick_blocks(selector, blocks):
    picked = jnp.einsum(
        "gb,dbi->dgi", selector.astype(jnp.bfloat16), blocks, preferred_element_type=jnp.float32
    )
    return picked.astype(jnp.bfloat16)


def per_device(src_emb, tgt_emb, src_hidden, growth, tgt_mass, pair_code, pair_count, block_batch):
    feat_width = src_emb.shape[0]
    src_blocks = src_emb.shape[1] // BLK
    tgt_blocks = tgt_emb.shape[1] // BLK
    src_cells = src_blocks * BLK
    tgt_cells = tgt_blocks * BLK
    slot_count = pair_code.shape[2]
    group_size = math.gcd(slot_count, 64)
    group_count = slot_count // group_size
    pair_slots = pair_code.reshape(slot_count)
    alive_mask = (jnp.arange(slot_count, dtype=jnp.int32) < pair_count.reshape(())).astype(
        jnp.float32
    )
    src_ids = pair_slots // tgt_blocks
    tgt_ids = pair_slots % tgt_blocks
    src_select = (src_ids[:, None] == jnp.arange(src_blocks, dtype=jnp.int32)[None, :]).astype(
        jnp.float32
    )
    tgt_select = (tgt_ids[:, None] == jnp.arange(tgt_blocks, dtype=jnp.int32)[None, :]).astype(
        jnp.float32
    )
    x_blocks = src_emb.reshape(feat_width, src_blocks, BLK)
    y_blocks = tgt_emb.reshape(feat_width, tgt_blocks, BLK)
    x_norms = jnp.sum(jnp.square(x_blocks.astype(jnp.float32)), axis=0)
    y_norms = jnp.sum(jnp.square(y_blocks.astype(jnp.float32)), axis=0)
    src_sel_groups = src_select.reshape(group_count, group_size, src_blocks)
    tgt_sel_groups = tgt_select.reshape(group_count, group_size, tgt_blocks)

    def kernel_group(inputs):
        src_sel, tgt_sel, alive_group = inputs
        x_part = pick_blocks(src_sel, x_blocks)
        y_part = pick_blocks(tgt_sel, y_blocks)
        inner_prods = jnp.einsum("dgi,dgj->gij", x_part, y_part, preferred_element_type=jnp.float32)
        x_sq = jnp.dot(src_sel, x_norms, precision=highest)
        y_sq = jnp.dot(tgt_sel, y_norms, precision=highest)
        distance = (x_sq[:, :, None] + y_sq[:, None, :] - 2.0 * inner_prods) / feat_width
        return jnp.exp(-distance / entropy_scale) * alive_group[:, None, None]

    kernel = lax.map(
        kernel_group, (src_sel_groups, tgt_sel_groups, alive_mask.reshape(group_count, group_size))
    )
    kernel = kernel.reshape(slot_count, BLK, BLK)
    src_mass = jnp.exp(growth)
    src_scale = jnp.ones((src_cells,), jnp.float32)
    tgt_scale = jnp.ones((tgt_cells,), jnp.float32)
    for iteration in range(ITERS):
        tgt_picked = jnp.dot(tgt_select, tgt_scale.reshape(tgt_blocks, BLK), precision=highest)
        src_picked = jnp.dot(src_select, src_scale.reshape(src_blocks, BLK), precision=highest)
        row_slots = jnp.einsum("pij,pj->pi", kernel, tgt_picked, precision=highest)
        col_slots = jnp.einsum("pij,pi->pj", kernel, src_picked, precision=highest)
        row_part = jnp.dot(src_select.T, row_slots, precision=highest).reshape(src_cells)
        col_part = jnp.dot(tgt_select.T, col_slots, precision=highest).reshape(tgt_cells)
        row_sums = lax.psum(row_part, "tgt")
        col_sums = lax.psum(col_part, "src")
        src_scale, tgt_scale = (
            rescale(src_scale, src_mass, row_sums),
            rescale(tgt_scale, tgt_mass, col_sums),
        )
    src_potential = entropy_scale * jnp.log(src_scale)
    tgt_potential = entropy_scale * jnp.log(tgt_scale)
    src_blocked = src_scale.reshape(src_blocks, BLK)
    tgt_blocked = tgt_scale.reshape(tgt_blocks, BLK)

    def gradient_group(carry, inputs):
        dx_total, dy_total = carry
        src_sel, tgt_sel, kernel_part = inputs
        row_scale = jnp.dot(src_sel, src_blocked, precision=highest)
        col_scale = jnp.dot(tgt_sel, tgt_blocked, precision=highest)
        transport = row_scale[:, :, None] * kernel_part * col_scale[:, None, :]
        plan_bf16 = transport.astype(jnp.bfloat16)
        x_part = pick_blocks(src_sel, x_blocks)
        y_part = pick_blocks(tgt_sel, y_blocks)
        pulled = jnp.einsum("gij,dgj->dgi", plan_bf16, y_part, preferred_element_type=jnp.float32)
        pushed = jnp.einsum("gij,dgi->dgj", plan_bf16, x_part, preferred_element_type=jnp.float32)
        dx_term = jnp.sum(transport, axis=2)[None] * x_part.astype(jnp.float32) - pulled
        dy_term = jnp.sum(transport, axis=1)[None] * y_part.astype(jnp.float32) - pushed
        dx_total = dx_total + jnp.einsum("gb,dgi->dbi", src_sel, dx_term, precision=highest)
        dy_total = dy_total + jnp.einsum("gb,dgi->dbi", tgt_sel, dy_term, precision=highest)
        return ((dx_total, dy_total), None)

    start_grads = (
        jnp.zeros((feat_width, src_blocks, BLK), jnp.float32),
        jnp.zeros((feat_width, tgt_blocks, BLK), jnp.float32),
    )
    (dx_total, dy_total), _ = lax.scan(
        gradient_group,
        start_grads,
        (src_sel_groups, tgt_sel_groups, kernel.reshape(group_count, group_size, BLK, BLK)),
    )
    tgt_grad = lax.psum(dy_total.reshape(feat_width, tgt_cells), "src")
    hidden_blocks = src_hidden.reshape(feat_width, src_blocks, BLK)
    grad_share = lax.psum_scatter(dx_total, "tgt", scatter_dimension=1, tiled=True)
    share_blocks = grad_share.shape[1]
    first_block = lax.axis_index("tgt") * share_blocks
    hidden_share = lax.dynamic_slice_in_dim(hidden_blocks, first_block, share_blocks, 1)
    batch_share = lax.dynamic_slice_in_dim(block_batch, first_block, share_blocks, 0)
    outer = (
        jnp.einsum("dbi,ebi->bde", hidden_share.astype(jnp.float32), grad_share, precision=highest)
        / BLK
    )
    wanted = jnp.arange(ENC_DEV * lax.axis_size(("src", "tgt")), dtype=jnp.int32)
    owners = (batch_share[None, :] == wanted[:, None]).astype(jnp.float32)
    adapter_grad = lax.psum_scatter(
        jnp.einsum("kb,bde->kde", owners, outer, precision=highest),
        ("src", "tgt"),
        scatter_dimension=0,
        tiled=True,
    )
    return (src_potential, tgt_potential, tgt_grad, adapter_grad)


def solution(mesh):
    in_specs = (
        P(None, "src"),
        P(None, "tgt"),
        P(None, "src"),
        P("src"),
        P("tgt"),
        P("src", "tgt", None),
        P("src", "tgt"),
        P("src"),
    )
    out_specs = (P("src"), P("tgt"), P(None, "tgt"), P(("src", "tgt"), None, None))
    return jax.shard_map(
        per_device, mesh=mesh, in_specs=in_specs, out_specs=out_specs, check_vma=False
    )
```

profile of v0, /device:TPU:0, one launch (start us, length us, event | category | flops | bytes accessed | tf_op | source)
XLA Modules:
  0.0 1027.3 jit_solution(16935787503366914984)
XLA Ops:
  17.6 84.6 %while.23 = (s32[]{:T(128)}, f32[8,64,128,128]{3,2,1,0:T(8,128)}, f32[8,64,128]{2,1,0:T(8,128)S(1)}, f32[128,128]{1,0:T(8,128)S(1)}, f32[8,64,128]{2,1,0:T(8,128...) while((s32[]{:T(128)}, f32[8,64,128,128]{3,2,1,0:T(8,128)}, ...), condition=%wide.region_3.4_spmd, body=%wide.region_2.3_spmd.sunk | while | flops 435159040 | bytes 21334412 | solution.py:64
  21.5 6.6 bitcast_dynamic-update-slice_fusion.2
  32.1 6.6 bitcast_dynamic-update-slice_fusion.2
  42.7 6.6 bitcast_dynamic-update-slice_fusion.2
  53.3 6.6 bitcast_dynamic-update-slice_fusion.2
  63.8 6.6 bitcast_dynamic-update-slice_fusion.2
  74.4 6.6 bitcast_dynamic-update-slice_fusion.2
  85.0 6.6 bitcast_dynamic-update-slice_fusion.2
  95.5 6.6 bitcast_dynamic-update-slice_fusion.2
  102.5 55.7 %fusion.97 = f32[512,1,128]{2,1,0:T(1,128)S(1)} fusion(f32[512,128,128]{2,1,0:T(8,128)} %bitcast.228, f32[512,128,1]{1,2,0:T(1,128)S(1)} %bitcast.246), kind=kOutput, calls=%fused_computation.137 | convolution fusion | flops 100663296 | bytes 34078720 | tf_op jit(solution)/shard_map/pij,pj->pi/dot_general | solution.py:74
  160.0 32.0 %fusion.98 = f32[512,1,128]{2,1,0:T(1,128)S(1)} fusion(f32[512,128,128]{2,1,0:T(8,128)} %bitcast.229, f32[512,128,1]{1,2,0:T(1,128)S(1)} %bitcast.248), kind=kOutput, calls=%fused_computation.138 | convolution fusion | flops 100663296 | bytes 34078720 | tf_op jit(solution)/shard_map/pij,pi->pj/dot_general | solution.py:75
  193.1 3.4 all-reduce.6.cloned.1.call-done
  197.7 32.3 %fusion.100 = f32[512,1,128]{2,1,0:T(1,128)S(1)} fusion(f32[512,128,128]{2,1,0:T(8,128)} %bitcast.230, f32[512,128,1]{1,2,0:T(1,128)S(1)} %bitcast.249), kind=kOutput, calls=%fused_computation.140 | convolution fusion | flops 100663296 | bytes 34078720 | tf_op jit(solution)/shard_map/pij,pi->pj/dot_general | solution.py:75
  231.3 53.3 %all-reduce.12.cloned.1.call-done = (f32[16384]{0:T(1024)}, f32[16384]{0:T(1024)}) async-done(((f32[16384]{0:T(1024)}, f32[16384]{0:T(1024)}), (f32[16384]{0:T(1024)}, f32[16384]{0:T(1024)})) %all-reduce.12.cloned.1.call-update) | async-done | bytes 131088 | tf_op jit(solution)/shard_map/psum | solution.py:79
  285.8 55.9 %fusion.99 = f32[512,1,128]{2,1,0:T(1,128)S(1)} fusion(f32[512,128,128]{2,1,0:T(8,128)} %bitcast.231, f32[512,128,1]{1,2,0:T(1,128)S(1)} %bitcast.247), kind=kOutput, calls=%fused_computation.139 | convolution fusion | flops 100663296 | bytes 34078720 | tf_op jit(solution)/shard_map/pij,pj->pi/dot_general | solution.py:74
  343.7 33.0 %all-reduce.8.cloned.1.call-done = f32[16384]{0:T(1024)} async-done(((f32[16384]{0:T(1024)}), f32[16384]{0:T(1024)}) %all-reduce.8.cloned.1.call-update) | async-done | bytes 65552 | tf_op jit(solution)/shard_map/psum | solution.py:78
  378.3 330.9 %while.24 = (s32[]{:T(128)}, f32[64,128,128]{1,2,0:T(8,128)}, f32[64,128,128]{1,2,0:T(8,128)}, f32[8,64,128]{2,1,0:T(8,128)S(1)}, f32[128,128]{1,0:T(8,128)}, /*...) while((s32[]{:T(128)}, f32[64,128,128]{1,2,0:T(8,128)}, ...), condition=%wide.region_11.12_spmd.clone, body=%wide.region_8.11_spmd.clone.sunk | while | flops 2191507456 | bytes 61508292 | solution.py:110
  381.0 5.4 fusion.193
  386.5 4.2 fusion.192
  392.9 10.6 %bitcast_add_fusion.5 = f32[64,128,128]{1,2,0:T(8,128)} fusion(f32[64,128,128]{1,2,0:T(8,128)} %get-tuple-element.360, f32[64,64,128]{2,1,0:T(8,128)} %fusion.193, bf16[64,64,128]{2,1,0:T(8,128)(2,1)} %fusion.187, pred[]{:T(512)S(6)} %compare.16, f32[64,128]{1,0:T(8,128)S(1)} %get-tuple-element.315, f32[8,64,128]{2,1,0:T(8,128)} %get-tuple-element.376, ...), kind=kOutput, calls=%fused_computation.23.clone.1 | convolution fusion | flops 808976384 | bytes 11600385 | tf_op jit(solution)/shard_map/while/body/eval_jaxpr/gb,dgi->dbi/dot_general | solution.py:103
  403.5 4.7 fusion.190
  408.2 9.7 bitcast_add_fusion.4
  420.5 5.4 fusion.193
  425.9 4.2 fusion.192
  432.3 11.2 %bitcast_add_fusion.5 = f32[64,128,128]{1,2,0:T(8,128)} fusion(f32[64,128,128]{1,2,0:T(8,128)} %get-tuple-element.360, f32[64,64,128]{2,1,0:T(8,128)} %fusion.193, bf16[64,64,128]{2,1,0:T(8,128)(2,1)} %fusion.187, pred[]{:T(512)S(6)} %compare.16, f32[64,128]{1,0:T(8,128)S(1)} %get-tuple-element.315, f32[8,64,128]{2,1,0:T(8,128)} %get-tuple-element.376, ...), kind=kOutput, calls=%fused_computation.23.clone.1 | convolution fusion | flops 808976384 | bytes 11600385 | tf_op jit(solution)/shard_map/while/body/eval_jaxpr/gb,dgi->dbi/dot_general | solution.py:103
  443.5 4.7 fusion.190
  448.2 11.3 %bitcast_add_fusion.4 = f32[64,128,128]{1,2,0:T(8,128)} fusion(f32[64,128,128]{1,2,0:T(8,128)} %get-tuple-element.359, f32[64,64,128]{2,1,0:T(8,128)S(1)} %fusion.190, bf16[64,64,128]{2,1,0:T(8,128)(2,1)S(1)} %fusion.191, pred[]{:T(512)S(6)} %compare.16, f32[64,128]{1,0:T(8,128)S(1)} %get-tuple-element.314, ...), kind=kOutput, calls=%fused_computation.24.clone.1 | convolution fusion | flops 808976384 | bytes 11599877 | tf_op jit(solution)/shard_map/while/body/eval_jaxpr/gb,dgi->dbi/dot_general | solution.py:102
  462.0 5.4 fusion.193
  467.5 4.2 fusion.192
  473.9 11.2 %bitcast_add_fusion.5 = f32[64,128,128]{1,2,0:T(8,128)} fusion(f32[64,128,128]{1,2,0:T(8,128)} %get-tuple-element.360, f32[64,64,128]{2,1,0:T(8,128)} %fusion.193, bf16[64,64,128]{2,1,0:T(8,128)(2,1)} %fusion.187, pred[]{:T(512)S(6)} %compare.16, f32[64,128]{1,0:T(8,128)S(1)} %get-tuple-element.315, f32[8,64,128]{2,1,0:T(8,128)} %get-tuple-element.376, ...), kind=kOutput, calls=%fused_computation.23.clone.1 | convolution fusion | flops 808976384 | bytes 11600385 | tf_op jit(solution)/shard_map/while/body/eval_jaxpr/gb,dgi->dbi/dot_general | solution.py:103
  485.1 4.7 fusion.190
  489.8 11.3 %bitcast_add_fusion.4 = f32[64,128,128]{1,2,0:T(8,128)} fusion(f32[64,128,128]{1,2,0:T(8,128)} %get-tuple-element.359, f32[64,64,128]{2,1,0:T(8,128)S(1)} %fusion.190, bf16[64,64,128]{2,1,0:T(8,128)(2,1)S(1)} %fusion.191, pred[]{:T(512)S(6)} %compare.16, f32[64,128]{1,0:T(8,128)S(1)} %get-tuple-element.314, ...), kind=kOutput, calls=%fused_computation.24.clone.1 | convolution fusion | flops 808976384 | bytes 11599877 | tf_op jit(solution)/shard_map/while/body/eval_jaxpr/gb,dgi->dbi/dot_general | solution.py:102
  503.6 5.4 fusion.193
  509.0 4.2 fusion.192
  515.5 11.2 %bitcast_add_fusion.5 = f32[64,128,128]{1,2,0:T(8,128)} fusion(f32[64,128,128]{1,2,0:T(8,128)} %get-tuple-element.360, f32[64,64,128]{2,1,0:T(8,128)} %fusion.193, bf16[64,64,128]{2,1,0:T(8,128)(2,1)} %fusion.187, pred[]{:T(512)S(6)} %compare.16, f32[64,128]{1,0:T(8,128)S(1)} %get-tuple-element.315, f32[8,64,128]{2,1,0:T(8,128)} %get-tuple-element.376, ...), kind=kOutput, calls=%fused_computation.23.clone.1 | convolution fusion | flops 808976384 | bytes 11600385 | tf_op jit(solution)/shard_map/while/body/eval_jaxpr/gb,dgi->dbi/dot_general | solution.py:103
  526.7 4.7 fusion.190
  531.4 11.3 %bitcast_add_fusion.4 = f32[64,128,128]{1,2,0:T(8,128)} fusion(f32[64,128,128]{1,2,0:T(8,128)} %get-tuple-element.359, f32[64,64,128]{2,1,0:T(8,128)S(1)} %fusion.190, bf16[64,64,128]{2,1,0:T(8,128)(2,1)S(1)} %fusion.191, pred[]{:T(512)S(6)} %compare.16, f32[64,128]{1,0:T(8,128)S(1)} %get-tuple-element.314, ...), kind=kOutput, calls=%fused_computation.24.clone.1 | convolution fusion | flops 808976384 | bytes 11599877 | tf_op jit(solution)/shard_map/while/body/eval_jaxpr/gb,dgi->dbi/dot_general | solution.py:102
  545.2 5.4 fusion.193
  550.6 4.2 fusion.192
  557.0 11.2 %bitcast_add_fusion.5 = f32[64,128,128]{1,2,0:T(8,128)} fusion(f32[64,128,128]{1,2,0:T(8,128)} %get-tuple-element.360, f32[64,64,128]{2,1,0:T(8,128)} %fusion.193, bf16[64,64,128]{2,1,0:T(8,128)(2,1)} %fusion.187, pred[]{:T(512)S(6)} %compare.16, f32[64,128]{1,0:T(8,128)S(1)} %get-tuple-element.315, f32[8,64,128]{2,1,0:T(8,128)} %get-tuple-element.376, ...), kind=kOutput, calls=%fused_computation.23.clone.1 | convolution fusion | flops 808976384 | bytes 11600385 | tf_op jit(solution)/shard_map/while/body/eval_jaxpr/gb,dgi->dbi/dot_general | solution.py:103
  568.2 4.7 fusion.190
  572.9 11.3 %bitcast_add_fusion.4 = f32[64,128,128]{1,2,0:T(8,128)} fusion(f32[64,128,128]{1,2,0:T(8,128)} %get-tuple-element.359, f32[64,64,128]{2,1,0:T(8,128)S(1)} %fusion.190, bf16[64,64,128]{2,1,0:T(8,128)(2,1)S(1)} %fusion.191, pred[]{:T(512)S(6)} %compare.16, f32[64,128]{1,0:T(8,128)S(1)} %get-tuple-element.314, ...), kind=kOutput, calls=%fused_computation.24.clone.1 | convolution fusion | flops 808976384 | bytes 11599877 | tf_op jit(solution)/shard_map/while/body/eval_jaxpr/gb,dgi->dbi/dot_general | solution.py:102
  586.7 5.4 fusion.193
  592.2 4.2 fusion.192
  598.6 11.2 %bitcast_add_fusion.5 = f32[64,128,128]{1,2,0:T(8,128)} fusion(f32[64,128,128]{1,2,0:T(8,128)} %get-tuple-element.360, f32[64,64,128]{2,1,0:T(8,128)} %fusion.193, bf16[64,64,128]{2,1,0:T(8,128)(2,1)} %fusion.187, pred[]{:T(512)S(6)} %compare.16, f32[64,128]{1,0:T(8,128)S(1)} %get-tuple-element.315, f32[8,64,128]{2,1,0:T(8,128)} %get-tuple-element.376, ...), kind=kOutput, calls=%fused_computation.23.clone.1 | convolution fusion | flops 808976384 | bytes 11600385 | tf_op jit(solution)/shard_map/while/body/eval_jaxpr/gb,dgi->dbi/dot_general | solution.py:103
  609.8 4.7 fusion.190
  614.5 11.3 %bitcast_add_fusion.4 = f32[64,128,128]{1,2,0:T(8,128)} fusion(f32[64,128,128]{1,2,0:T(8,128)} %get-tuple-element.359, f32[64,64,128]{2,1,0:T(8,128)S(1)} %fusion.190, bf16[64,64,128]{2,1,0:T(8,128)(2,1)S(1)} %fusion.191, pred[]{:T(512)S(6)} %compare.16, f32[64,128]{1,0:T(8,128)S(1)} %get-tuple-element.314, ...), kind=kOutput, calls=%fused_computation.24.clone.1 | convolution fusion | flops 808976384 | bytes 11599877 | tf_op jit(solution)/shard_map/while/body/eval_jaxpr/gb,dgi->dbi/dot_general | solution.py:102
  628.3 5.4 fusion.193
  633.7 4.2 fusion.192
  640.2 11.2 %bitcast_add_fusion.5 = f32[64,128,128]{1,2,0:T(8,128)} fusion(f32[64,128,128]{1,2,0:T(8,128)} %get-tuple-element.360, f32[64,64,128]{2,1,0:T(8,128)} %fusion.193, bf16[64,64,128]{2,1,0:T(8,128)(2,1)} %fusion.187, pred[]{:T(512)S(6)} %compare.16, f32[64,128]{1,0:T(8,128)S(1)} %get-tuple-element.315, f32[8,64,128]{2,1,0:T(8,128)} %get-tuple-element.376, ...), kind=kOutput, calls=%fused_computation.23.clone.1 | convolution fusion | flops 808976384 | bytes 11600385 | tf_op jit(solution)/shard_map/while/body/eval_jaxpr/gb,dgi->dbi/dot_general | solution.py:103
  651.4 4.7 fusion.190
  656.1 11.3 %bitcast_add_fusion.4 = f32[64,128,128]{1,2,0:T(8,128)} fusion(f32[64,128,128]{1,2,0:T(8,128)} %get-tuple-element.359, f32[64,64,128]{2,1,0:T(8,128)S(1)} %fusion.190, bf16[64,64,128]{2,1,0:T(8,128)(2,1)S(1)} %fusion.191, pred[]{:T(512)S(6)} %compare.16, f32[64,128]{1,0:T(8,128)S(1)} %get-tuple-element.314, ...), kind=kOutput, calls=%fused_computation.24.clone.1 | convolution fusion | flops 808976384 | bytes 11599877 | tf_op jit(solution)/shard_map/while/body/eval_jaxpr/gb,dgi->dbi/dot_general | solution.py:102
  669.9 5.4 fusion.193
  675.3 4.2 fusion.192
  681.7 11.2 %bitcast_add_fusion.5 = f32[64,128,128]{1,2,0:T(8,128)} fusion(f32[64,128,128]{1,2,0:T(8,128)} %get-tuple-element.360, f32[64,64,128]{2,1,0:T(8,128)} %fusion.193, bf16[64,64,128]{2,1,0:T(8,128)(2,1)} %fusion.187, pred[]{:T(512)S(6)} %compare.16, f32[64,128]{1,0:T(8,128)S(1)} %get-tuple-element.315, f32[8,64,128]{2,1,0:T(8,128)} %get-tuple-element.376, ...), kind=kOutput, calls=%fused_computation.23.clone.1 | convolution fusion | flops 808976384 | bytes 11600385 | tf_op jit(solution)/shard_map/while/body/eval_jaxpr/gb,dgi->dbi/dot_general | solution.py:103
  693.0 4.7 fusion.190
  697.7 11.3 %bitcast_add_fusion.4 = f32[64,128,128]{1,2,0:T(8,128)} fusion(f32[64,128,128]{1,2,0:T(8,128)} %get-tuple-element.359, f32[64,64,128]{2,1,0:T(8,128)S(1)} %fusion.190, bf16[64,64,128]{2,1,0:T(8,128)(2,1)S(1)} %fusion.191, pred[]{:T(512)S(6)} %compare.16, f32[64,128]{1,0:T(8,128)S(1)} %get-tuple-element.314, ...), kind=kOutput, calls=%fused_computation.24.clone.1 | convolution fusion | flops 808976384 | bytes 11599877 | tf_op jit(solution)/shard_map/while/body/eval_jaxpr/gb,dgi->dbi/dot_general | solution.py:102
  709.1 5.4 copy.15
  714.6 5.6 copy.14
  720.2 6.9 copy.62
  729.5 61.7 %reduce-scatter.3.cloned.1.call-done = f32[64,32,128]{2,0,1:T(8,128)} async-done(((f32[64,128,128]{2,0,1:T(8,128)}), f32[64,32,128]{2,0,1:T(8,128)}) %reduce-scatter.3.cloned.1.call-update) | async-done | bytes 1048592 | tf_op jit(solution)/shard_map/reduce_scatter | solution.py:117
  796.3 79.4 %all-reduce.10.cloned.1.call-done = f32[64,16384]{1,0:T(8,128)} async-done(((f32[64,16384]{1,0:T(8,128)}), f32[64,16384]{1,0:T(8,128)}) %all-reduce.10.cloned.1.call-update) | async-done | bytes 4194320 | tf_op jit(solution)/shard_map/psum | solution.py:115
  875.7 139.8 %reduce-scatter.5.cloned.1.call-done = f32[1,64,64]{2,1,0:T(8,128)} async-done(((f32[32,64,64]{2,1,0:T(8,128)}), f32[1,64,64]{2,1,0:T(8,128)}) %reduce-scatter.5.cloned.1.call-update) | async-done | bytes 16400 | tf_op jit(solution)/shard_map/reduce_scatter | solution.py:128
  1015.5 4.5 copy.97
  (178 shorter events, 96.2 us)
Async XLA Ops:
  7.2 189.4 %all-reduce.6.cloned.1.call-start = ((), (), s32[]{:S(2)}) async-start(), calls=%async_computation.2 | async-start | bytes 131072 | tf_op jit(solution)/shard_map/psum | solution.py:78
  9.2 4.4 copy-start.3
  17.6 84.6 %copy-start.9 = (s32[1,1,512]{2,1,0:T(1,128)S(1)}, s32[1,1,512]{2,1,0:T(1,128)}, u32[]{:S(2)}) copy-start(s32[1,1,512]{2,1,0:T(1,128)} %param.17) | copy-start | bytes 6148
  17.6 1.6 copy-start
  28.1 1.6 copy-start
  38.7 1.6 copy-start
  49.3 1.6 copy-start
  59.9 1.6 copy-start
  70.4 1.6 copy-start
  81.0 1.6 copy-start
  91.6 1.6 copy-start
  159.4 125.2 %all-reduce.12.cloned.1.call-start = ((), (), s32[]{:S(2)}) async-start(), calls=%async_computation.7 | async-start | bytes 262144 | tf_op jit(solution)/shard_map/psum | solution.py:79
  160.0 36.6 %copy-start.5 = (f32[16384]{0:T(1024)S(1)}, f32[16384]{0:T(1024)}, u32[]{:S(2)}) copy-start(f32[16384]{0:T(1024)} %param.15) | copy-start | bytes 196612
  197.7 86.9 %copy-start.4 = (f32[16384]{0:T(1024)S(1)}, f32[16384]{0:T(1024)}, u32[]{:S(2)}) copy-start(f32[16384]{0:T(1024)} %param.16) | copy-start | bytes 196612
  231.2 145.4 %all-reduce.8.cloned.1.call-start = ((), (), s32[]{:S(2)}) async-start(), calls=%async_computation.3 | async-start | bytes 131072 | tf_op jit(solution)/shard_map/psum | solution.py:78
  285.8 57.1 %copy-start.7 = (f32[16384]{0:T(1024)S(1)}, f32[16384]{0:T(1024)}, u32[]{:S(2)}) copy-start(f32[16384]{0:T(1024)} %get-tuple-element.184) | copy-start | bytes 196612
  285.8 57.1 %copy-start.8 = (f32[16384]{0:T(1024)S(1)}, f32[16384]{0:T(1024)}, u32[]{:S(2)}) copy-start(f32[16384]{0:T(1024)} %get-tuple-element.185) | copy-start | bytes 196612
  285.8 90.9 %copy-start.6 = (f32[16384]{0:T(1024)S(1)}, f32[16384]{0:T(1024)}, u32[]{:S(2)}) copy-start(f32[16384]{0:T(1024)} %all-reduce.6.cloned.1.call-done) | copy-start | bytes 196612
  342.8 448.4 %reduce-scatter.3.cloned.1.call-start = ((), (), s32[]{:S(2)}) async-start(), calls=%async_computation.5 | async-start | bytes 5242880 | tf_op jit(solution)/shard_map/reduce_scatter | solution.py:117
  381.0 9.7 copy-start.1
  392.9 10.6 %copy-start.2 = (bf16[64,64,128]{2,1,0:T(8,128)(2,1)S(1)}, bf16[64,64,128]{2,1,0:T(8,128)(2,1)}, u32[]{:S(2)}) copy-start(bf16[64,64,128]{2,1,0:T(8,128)(2,1)} %fusion.187) | copy-start | bytes 3145732 | tf_op jit(solution)/shard_map/while
  420.4 9.7 copy-start.1
  432.3 11.2 %copy-start.2 = (bf16[64,64,128]{2,1,0:T(8,128)(2,1)S(1)}, bf16[64,64,128]{2,1,0:T(8,128)(2,1)}, u32[]{:S(2)}) copy-start(bf16[64,64,128]{2,1,0:T(8,128)(2,1)} %fusion.187) | copy-start | bytes 3145732 | tf_op jit(solution)/shard_map/while
  462.0 9.7 copy-start.1
  473.9 11.2 %copy-start.2 = (bf16[64,64,128]{2,1,0:T(8,128)(2,1)S(1)}, bf16[64,64,128]{2,1,0:T(8,128)(2,1)}, u32[]{:S(2)}) copy-start(bf16[64,64,128]{2,1,0:T(8,128)(2,1)} %fusion.187) | copy-start | bytes 3145732 | tf_op jit(solution)/shard_map/while
  503.6 9.7 copy-start.1
  515.5 11.2 %copy-start.2 = (bf16[64,64,128]{2,1,0:T(8,128)(2,1)S(1)}, bf16[64,64,128]{2,1,0:T(8,128)(2,1)}, u32[]{:S(2)}) copy-start(bf16[64,64,128]{2,1,0:T(8,128)(2,1)} %fusion.187) | copy-start | bytes 3145732 | tf_op jit(solution)/shard_map/while
  545.2 9.7 copy-start.1
  557.0 11.2 %copy-start.2 = (bf16[64,64,128]{2,1,0:T(8,128)(2,1)S(1)}, bf16[64,64,128]{2,1,0:T(8,128)(2,1)}, u32[]{:S(2)}) copy-start(bf16[64,64,128]{2,1,0:T(8,128)(2,1)} %fusion.187) | copy-start | bytes 3145732 | tf_op jit(solution)/shard_map/while
  586.7 9.7 copy-start.1
  598.6 11.2 %copy-start.2 = (bf16[64,64,128]{2,1,0:T(8,128)(2,1)S(1)}, bf16[64,64,128]{2,1,0:T(8,128)(2,1)}, u32[]{:S(2)}) copy-start(bf16[64,64,128]{2,1,0:T(8,128)(2,1)} %fusion.187) | copy-start | bytes 3145732 | tf_op jit(solution)/shard_map/while
  628.3 9.7 copy-start.1
  640.2 11.2 %copy-start.2 = (bf16[64,64,128]{2,1,0:T(8,128)(2,1)S(1)}, bf16[64,64,128]{2,1,0:T(8,128)(2,1)}, u32[]{:S(2)}) copy-start(bf16[64,64,128]{2,1,0:T(8,128)(2,1)} %fusion.187) | copy-start | bytes 3145732 | tf_op jit(solution)/shard_map/while
  669.9 9.7 copy-start.1
  681.7 11.2 %copy-start.2 = (bf16[64,64,128]{2,1,0:T(8,128)(2,1)S(1)}, bf16[64,64,128]{2,1,0:T(8,128)(2,1)}, u32[]{:S(2)}) copy-start(bf16[64,64,128]{2,1,0:T(8,128)(2,1)} %fusion.187) | copy-start | bytes 3145732 | tf_op jit(solution)/shard_map/while
  714.6 161.1 %all-reduce.10.cloned.1.call-start = ((), (), s32[]{:S(2)}) async-start(), calls=%async_computation.4 | async-start | bytes 8388608 | tf_op jit(solution)/shard_map/psum | solution.py:115
  727.1 2.3 copy-start.10
  727.2 288.3 %reduce-scatter.5.cloned.1.call-start = ((), (), s32[]{:S(2)}) async-start(), calls=%async_computation.6 | async-start | bytes 1081344 | tf_op jit(solution)/shard_map/reduce_scatter | solution.py:128
Sparse Core Ops, SparseCore 0:
  159.5 36.9 all-reduce.5
  231.4 53.2 all-reduce.11
  343.0 33.6 all-reduce.7
  714.7 76.4 reduce-scatter.2
  794.3 81.3 all-reduce.9
  878.4 137.0 reduce-scatter.4
where the time goes:
time: 1040 us; the launch traced here: 1030 us
  matrix products  558 us (54%)
  waiting for transfers between devices  371 us (36%)
  other arithmetic  41.4 us (4%)
  local copies, waits for them, and re-layouts  40.3 us (4%)
  between operations  15.4 us (1%)
    reduce_scatter x1, waiting for transfers between devices, per_device(): lax.psum_scatter(jnp.einsum('kb,bde->kde', owners, outer, precision=highe...  140 us
    dot_general x2, matrix products, per_device(): row_slots = jnp.einsum('pij,pj->pi', kernel, tgt_picked, precision=highest)  112 us
    dot_general x8, matrix products, gradient_group(): jnp.einsum('gb,dgi->dbi', tgt_sel, dy_term, precision=highest)  89 us
    dot_general x8, matrix products, gradient_group(): jnp.einsum('gb,dgi->dbi', src_sel, dx_term, precision=highest)  88.5 us
    psum x1, waiting for transfers between devices, per_device(): tgt_grad = lax.psum(dy_total.reshape(feat_width, tgt_cells), 'src')  79.4 us
    dot_general x2, matrix products, per_device(): col_slots = jnp.einsum('pij,pi->pj', kernel, src_picked, precision=highest)  64.3 us
    reduce_scatter x1, waiting for transfers between devices, per_device(): lax.psum_scatter(dx_total, 'tgt', scatter_dimension=1, tiled=True)  61.7 us
    psum x1, waiting for transfers between devices, per_device(): col_sums = lax.psum(col_part, 'src')  53.3 us
  transfers between devices with their start and end apart: 6, of which 6 were waited for; matrix products, arithmetic and copies ran while one was open for 5% of the time, Pallas kernels for 0%

commit v1 on v0

--- a/solution.py
+++ b/solution.py
@@ -76,7 +76,11 @@
         row_part = jnp.dot(src_select.T, row_slots, precision=highest).reshape(src_cells)
         col_part = jnp.dot(tgt_select.T, col_slots, precision=highest).reshape(tgt_cells)
         row_sums = lax.psum(row_part, "tgt")
-        col_sums = lax.psum(col_part, "src")
+        col_sums = col_part
+        for hop in (1, 2, 4):
+            col_sums = col_sums + lax.ppermute(
+                col_sums, "src", [(dev, dev ^ hop) for dev in range(8)]
+            )
         src_scale, tgt_scale = (
             rescale(src_scale, src_mass, row_sums),
             rescale(tgt_scale, tgt_mass, col_sums),

time: 1040 us -> 999 us (0.961)
  waiting for transfers between devices: 371 us -> 325 us
    psum x1 -> x0, waiting for transfers between devices: 53.3 us -> none  [per_device(): col_sums = lax.psum(col_part, 'src')]
    psum x2 -> x1, waiting for transfers between devices: 36.4 us -> 35.1 us  [per_device(): row_sums = lax.psum(row_part, 'tgt')]
  transfers between devices with their start and end apart: 6 -> 10, of which waited for: 6 -> 9; matrix products, arithmetic and copies ran while one was open for 5% -> 8% of each run, Pallas kernels for 0% -> 0%
where the time goes in v1:
time: 999 us; the launch traced here: 986 us
  matrix products  556 us (56%)
  waiting for transfers between devices  325 us (33%)
  other arithmetic  40.6 us (4%)
  local copies, waits for them, and re-layouts  40.4 us (4%)
  between operations  15.1 us (2%)
    reduce_scatter x1, waiting for transfers between devices, per_device(): lax.psum_scatter(jnp.einsum('kb,bde->kde', owners, outer, precision=highe...  140 us
    dot_general x2, matrix products, per_device(): row_slots = jnp.einsum('pij,pj->pi', kernel, tgt_picked, precision=highest)  112 us
    dot_general x8, matrix products, gradient_group(): jnp.einsum('gb,dgi->dbi', tgt_sel, dy_term, precision=highest)  89.1 us
    dot_general x8, matrix products, gradient_group(): jnp.einsum('gb,dgi->dbi', src_sel, dx_term, precision=highest)  88.5 us
    psum x1, waiting for transfers between devices, per_device(): tgt_grad = lax.psum(dy_total.reshape(feat_width, tgt_cells), 'src')  79.5 us
    dot_general x2, matrix products, per_device(): col_slots = jnp.einsum('pij,pi->pj', kernel, src_picked, precision=highest)  64 us
    reduce_scatter x1, waiting for transfers between devices, per_device(): lax.psum_scatter(dx_total, 'tgt', scatter_dimension=1, tiled=True)  61.7 us
    dot_general x8, matrix products, kernel_group(): jnp.einsum('dgi,dgj->gij', x_part, y_part, preferred_element_type=jnp.flo...  53 us
  transfers between devices with their start and end apart: 10, of which 9 were waited for; matrix products, arithmetic and copies ran while one was open for 8% of the time, Pallas kernels for 0%

profile of v1, /device:TPU:0, one launch (start us, length us, event | category | flops | bytes accessed | tf_op | source)
XLA Modules:
  0.0 986.2 jit_solution(5025419893124097393)
XLA Ops:
  17.6 84.6 %while.23 = (s32[]{:T(128)}, f32[8,64,128,128]{3,2,1,0:T(8,128)}, f32[8,64,128]{2,1,0:T(8,128)S(1)}, f32[128,128]{1,0:T(8,128)S(1)}, f32[8,64,128]{2,1,0:T(8,128...) while((s32[]{:T(128)}, f32[8,64,128,128]{3,2,1,0:T(8,128)}, ...), condition=%wide.region_3.4_spmd, body=%wide.region_2.3_spmd.sunk | while | flops 435159040 | bytes 21334412 | solution.py:64
  21.5 6.6 bitcast_dynamic-update-slice_fusion.2
  32.1 6.6 bitcast_dynamic-update-slice_fusion.2
  42.7 6.6 bitcast_dynamic-update-slice_fusion.2
  53.3 6.6 bitcast_dynamic-update-slice_fusion.2
  63.8 6.6 bitcast_dynamic-update-slice_fusion.2
  74.4 6.6 bitcast_dynamic-update-slice_fusion.2
  85.0 6.6 bitcast_dynamic-update-slice_fusion.2
  95.5 6.6 bitcast_dynamic-update-slice_fusion.2
  102.5 31.9 %fusion.97 = f32[512,1,128]{2,1,0:T(1,128)S(1)} fusion(f32[512,128,128]{2,1,0:T(8,128)} %bitcast.228, f32[512,128,1]{1,2,0:T(1,128)S(1)} %bitcast.248), kind=kOutput, calls=%fused_computation.137 | convolution fusion | flops 100663296 | bytes 34078720 | tf_op jit(solution)/shard_map/pij,pi->pj/dot_general | solution.py:75
  136.4 2.9 collective-permute-start.1
  139.3 55.9 %fusion.96 = f32[512,1,128]{2,1,0:T(1,128)S(1)} fusion(f32[512,128,128]{2,1,0:T(8,128)} %bitcast.229, f32[512,128,1]{1,2,0:T(1,128)S(1)} %bitcast.247), kind=kOutput, calls=%fused_computation.136 | convolution fusion | flops 100663296 | bytes 34078720 | tf_op jit(solution)/shard_map/pij,pj->pi/dot_general | solution.py:74
  199.9 56.1 %fusion.98 = f32[512,1,128]{2,1,0:T(1,128)S(1)} fusion(f32[512,128,128]{2,1,0:T(8,128)} %bitcast.230, f32[512,128,1]{1,2,0:T(1,128)S(1)} %bitcast.246), kind=kOutput, calls=%fused_computation.138 | convolution fusion | flops 100663296 | bytes 34078720 | tf_op jit(solution)/shard_map/pij,pj->pi/dot_general | solution.py:74
  257.2 35.1 %all-reduce.6.cloned.1.call-done = (f32[16384]{0:T(1024)}, f32[16384]{0:T(1024)}) async-done(((f32[16384]{0:T(1024)}, f32[16384]{0:T(1024)}), (f32[16384]{0:T(1024)}, f32[16384]{0:T(1024)})) %all-reduce.6.cloned.1.call-update) | async-done | bytes 131088 | tf_op jit(solution)/shard_map/psum | solution.py:78
  293.6 32.1 %fusion.99 = f32[512,1,128]{2,1,0:T(1,128)S(1)} fusion(f32[512,128,128]{2,1,0:T(8,128)} %bitcast.231, f32[512,128,1]{1,2,0:T(1,128)S(1)} %bitcast.249), kind=kOutput, calls=%fused_computation.139 | convolution fusion | flops 100663296 | bytes 34078720 | tf_op jit(solution)/shard_map/pij,pi->pj/dot_general | solution.py:75
  329.0 2.8 collective-permute-done.4
  337.0 331.1 %while.24 = (s32[]{:T(128)}, f32[64,128,128]{1,2,0:T(8,128)}, f32[64,128,128]{1,2,0:T(8,128)}, f32[8,64,128]{2,1,0:T(8,128)S(1)}, f32[128,128]{1,0:T(8,128)}, /*...) while((s32[]{:T(128)}, f32[64,128,128]{1,2,0:T(8,128)}, ...), condition=%wide.region_9.10_spmd.clone, body=%wide.region_6.9_spmd.clone.sunk | while | flops 2191507456 | bytes 61508292 | solution.py:114
  339.7 5.4 fusion.192
  345.1 4.2 fusion.191
  351.6 10.6 %bitcast_add_fusion.5 = f32[64,128,128]{1,2,0:T(8,128)} fusion(f32[64,128,128]{1,2,0:T(8,128)} %get-tuple-element.360, f32[64,64,128]{2,1,0:T(8,128)} %fusion.192, bf16[64,64,128]{2,1,0:T(8,128)(2,1)} %fusion.186, pred[]{:T(512)S(6)} %compare.16, f32[64,128]{1,0:T(8,128)S(1)} %get-tuple-element.315, f32[8,64,128]{2,1,0:T(8,128)} %get-tuple-element.376, ...), kind=kOutput, calls=%fused_computation.23.clone.1 | convolution fusion | flops 808976384 | bytes 11600385 | tf_op jit(solution)/shard_map/while/body/eval_jaxpr/gb,dgi->dbi/dot_general | solution.py:107
  362.2 4.7 fusion.189
  366.9 9.7 bitcast_add_fusion.4
  379.2 5.4 fusion.192
  384.6 4.2 fusion.191
  391.0 11.2 %bitcast_add_fusion.5 = f32[64,128,128]{1,2,0:T(8,128)} fusion(f32[64,128,128]{1,2,0:T(8,128)} %get-tuple-element.360, f32[64,64,128]{2,1,0:T(8,128)} %fusion.192, bf16[64,64,128]{2,1,0:T(8,128)(2,1)} %fusion.186, pred[]{:T(512)S(6)} %compare.16, f32[64,128]{1,0:T(8,128)S(1)} %get-tuple-element.315, f32[8,64,128]{2,1,0:T(8,128)} %get-tuple-element.376, ...), kind=kOutput, calls=%fused_computation.23.clone.1 | convolution fusion | flops 808976384 | bytes 11600385 | tf_op jit(solution)/shard_map/while/body/eval_jaxpr/gb,dgi->dbi/dot_general | solution.py:107
  402.3 4.7 fusion.189
  407.0 11.3 %bitcast_add_fusion.4 = f32[64,128,128]{1,2,0:T(8,128)} fusion(f32[64,128,128]{1,2,0:T(8,128)} %get-tuple-element.359, f32[64,64,128]{2,1,0:T(8,128)S(1)} %fusion.189, bf16[64,64,128]{2,1,0:T(8,128)(2,1)S(1)} %fusion.190, pred[]{:T(512)S(6)} %compare.16, f32[64,128]{1,0:T(8,128)S(1)} %get-tuple-element.314, ...), kind=kOutput, calls=%fused_computation.24.clone.1 | convolution fusion | flops 808976384 | bytes 11599877 | tf_op jit(solution)/shard_map/while/body/eval_jaxpr/gb,dgi->dbi/dot_general | solution.py:106
  420.7 5.4 fusion.192
  426.2 4.2 fusion.191
  432.6 11.2 %bitcast_add_fusion.5 = f32[64,128,128]{1,2,0:T(8,128)} fusion(f32[64,128,128]{1,2,0:T(8,128)} %get-tuple-element.360, f32[64,64,128]{2,1,0:T(8,128)} %fusion.192, bf16[64,64,128]{2,1,0:T(8,128)(2,1)} %fusion.186, pred[]{:T(512)S(6)} %compare.16, f32[64,128]{1,0:T(8,128)S(1)} %get-tuple-element.315, f32[8,64,128]{2,1,0:T(8,128)} %get-tuple-element.376, ...), kind=kOutput, calls=%fused_computation.23.clone.1 | convolution fusion | flops 808976384 | bytes 11600385 | tf_op jit(solution)/shard_map/while/body/eval_jaxpr/gb,dgi->dbi/dot_general | solution.py:107
  443.8 4.7 fusion.189
  448.6 11.3 %bitcast_add_fusion.4 = f32[64,128,128]{1,2,0:T(8,128)} fusion(f32[64,128,128]{1,2,0:T(8,128)} %get-tuple-element.359, f32[64,64,128]{2,1,0:T(8,128)S(1)} %fusion.189, bf16[64,64,128]{2,1,0:T(8,128)(2,1)S(1)} %fusion.190, pred[]{:T(512)S(6)} %compare.16, f32[64,128]{1,0:T(8,128)S(1)} %get-tuple-element.314, ...), kind=kOutput, calls=%fused_computation.24.clone.1 | convolution fusion | flops 808976384 | bytes 11599877 | tf_op jit(solution)/shard_map/while/body/eval_jaxpr/gb,dgi->dbi/dot_general | solution.py:106
  462.3 5.4 fusion.192
  467.8 4.2 fusion.191
  474.2 11.2 %bitcast_add_fusion.5 = f32[64,128,128]{1,2,0:T(8,128)} fusion(f32[64,128,128]{1,2,0:T(8,128)} %get-tuple-element.360, f32[64,64,128]{2,1,0:T(8,128)} %fusion.192, bf16[64,64,128]{2,1,0:T(8,128)(2,1)} %fusion.186, pred[]{:T(512)S(6)} %compare.16, f32[64,128]{1,0:T(8,128)S(1)} %get-tuple-element.315, f32[8,64,128]{2,1,0:T(8,128)} %get-tuple-element.376, ...), kind=kOutput, calls=%fused_computation.23.clone.1 | convolution fusion | flops 808976384 | bytes 11600385 | tf_op jit(solution)/shard_map/while/body/eval_jaxpr/gb,dgi->dbi/dot_general | solution.py:107
  485.4 4.7 fusion.189
  490.2 11.3 %bitcast_add_fusion.4 = f32[64,128,128]{1,2,0:T(8,128)} fusion(f32[64,128,128]{1,2,0:T(8,128)} %get-tuple-element.359, f32[64,64,128]{2,1,0:T(8,128)S(1)} %fusion.189, bf16[64,64,128]{2,1,0:T(8,128)(2,1)S(1)} %fusion.190, pred[]{:T(512)S(6)} %compare.16, f32[64,128]{1,0:T(8,128)S(1)} %get-tuple-element.314, ...), kind=kOutput, calls=%fused_computation.24.clone.1 | convolution fusion | flops 808976384 | bytes 11599877 | tf_op jit(solution)/shard_map/while/body/eval_jaxpr/gb,dgi->dbi/dot_general | solution.py:106
  503.9 5.4 fusion.192
  509.4 4.2 fusion.191
  515.8 11.2 %bitcast_add_fusion.5 = f32[64,128,128]{1,2,0:T(8,128)} fusion(f32[64,128,128]{1,2,0:T(8,128)} %get-tuple-element.360, f32[64,64,128]{2,1,0:T(8,128)} %fusion.192, bf16[64,64,128]{2,1,0:T(8,128)(2,1)} %fusion.186, pred[]{:T(512)S(6)} %compare.16, f32[64,128]{1,0:T(8,128)S(1)} %get-tuple-element.315, f32[8,64,128]{2,1,0:T(8,128)} %get-tuple-element.376, ...), kind=kOutput, calls=%fused_computation.23.clone.1 | convolution fusion | flops 808976384 | bytes 11600385 | tf_op jit(solution)/shard_map/while/body/eval_jaxpr/gb,dgi->dbi/dot_general | solution.py:107
  527.0 4.7 fusion.189
  531.7 11.3 %bitcast_add_fusion.4 = f32[64,128,128]{1,2,0:T(8,128)} fusion(f32[64,128,128]{1,2,0:T(8,128)} %get-tuple-element.359, f32[64,64,128]{2,1,0:T(8,128)S(1)} %fusion.189, bf16[64,64,128]{2,1,0:T(8,128)(2,1)S(1)} %fusion.190, pred[]{:T(512)S(6)} %compare.16, f32[64,128]{1,0:T(8,128)S(1)} %get-tuple-element.314, ...), kind=kOutput, calls=%fused_computation.24.clone.1 | convolution fusion | flops 808976384 | bytes 11599877 | tf_op jit(solution)/shard_map/while/body/eval_jaxpr/gb,dgi->dbi/dot_general | solution.py:106
  545.5 5.4 fusion.192
  551.0 4.2 fusion.191
  557.4 11.2 %bitcast_add_fusion.5 = f32[64,128,128]{1,2,0:T(8,128)} fusion(f32[64,128,128]{1,2,0:T(8,128)} %get-tuple-element.360, f32[64,64,128]{2,1,0:T(8,128)} %fusion.192, bf16[64,64,128]{2,1,0:T(8,128)(2,1)} %fusion.186, pred[]{:T(512)S(6)} %compare.16, f32[64,128]{1,0:T(8,128)S(1)} %get-tuple-element.315, f32[8,64,128]{2,1,0:T(8,128)} %get-tuple-element.376, ...), kind=kOutput, calls=%fused_computation.23.clone.1 | convolution fusion | flops 808976384 | bytes 11600385 | tf_op jit(solution)/shard_map/while/body/eval_jaxpr/gb,dgi->dbi/dot_general | solution.py:107
  568.6 4.7 fusion.189
  573.3 11.3 %bitcast_add_fusion.4 = f32[64,128,128]{1,2,0:T(8,128)} fusion(f32[64,128,128]{1,2,0:T(8,128)} %get-tuple-element.359, f32[64,64,128]{2,1,0:T(8,128)S(1)} %fusion.189, bf16[64,64,128]{2,1,0:T(8,128)(2,1)S(1)} %fusion.190, pred[]{:T(512)S(6)} %compare.16, f32[64,128]{1,0:T(8,128)S(1)} %get-tuple-element.314, ...), kind=kOutput, calls=%fused_computation.24.clone.1 | convolution fusion | flops 808976384 | bytes 11599877 | tf_op jit(solution)/shard_map/while/body/eval_jaxpr/gb,dgi->dbi/dot_general | solution.py:106
  587.1 5.4 fusion.192
  592.6 4.2 fusion.191
  599.0 11.2 %bitcast_add_fusion.5 = f32[64,128,128]{1,2,0:T(8,128)} fusion(f32[64,128,128]{1,2,0:T(8,128)} %get-tuple-element.360, f32[64,64,128]{2,1,0:T(8,128)} %fusion.192, bf16[64,64,128]{2,1,0:T(8,128)(2,1)} %fusion.186, pred[]{:T(512)S(6)} %compare.16, f32[64,128]{1,0:T(8,128)S(1)} %get-tuple-element.315, f32[8,64,128]{2,1,0:T(8,128)} %get-tuple-element.376, ...), kind=kOutput, calls=%fused_computation.23.clone.1 | convolution fusion | flops 808976384 | bytes 11600385 | tf_op jit(solution)/shard_map/while/body/eval_jaxpr/gb,dgi->dbi/dot_general | solution.py:107
  610.2 4.7 fusion.189
  614.9 11.3 %bitcast_add_fusion.4 = f32[64,128,128]{1,2,0:T(8,128)} fusion(f32[64,128,128]{1,2,0:T(8,128)} %get-tuple-element.359, f32[64,64,128]{2,1,0:T(8,128)S(1)} %fusion.189, bf16[64,64,128]{2,1,0:T(8,128)(2,1)S(1)} %fusion.190, pred[]{:T(512)S(6)} %compare.16, f32[64,128]{1,0:T(8,128)S(1)} %get-tuple-element.314, ...), kind=kOutput, calls=%fused_computation.24.clone.1 | convolution fusion | flops 808976384 | bytes 11599877 | tf_op jit(solution)/shard_map/while/body/eval_jaxpr/gb,dgi->dbi/dot_general | solution.py:106
  628.7 5.4 fusion.192
  634.2 4.2 fusion.191
  640.6 11.2 %bitcast_add_fusion.5 = f32[64,128,128]{1,2,0:T(8,128)} fusion(f32[64,128,128]{1,2,0:T(8,128)} %get-tuple-element.360, f32[64,64,128]{2,1,0:T(8,128)} %fusion.192, bf16[64,64,128]{2,1,0:T(8,128)(2,1)} %fusion.186, pred[]{:T(512)S(6)} %compare.16, f32[64,128]{1,0:T(8,128)S(1)} %get-tuple-element.315, f32[8,64,128]{2,1,0:T(8,128)} %get-tuple-element.376, ...), kind=kOutput, calls=%fused_computation.23.clone.1 | convolution fusion | flops 808976384 | bytes 11600385 | tf_op jit(solution)/shard_map/while/body/eval_jaxpr/gb,dgi->dbi/dot_general | solution.py:107
  651.8 4.7 fusion.189
  656.5 11.3 %bitcast_add_fusion.4 = f32[64,128,128]{1,2,0:T(8,128)} fusion(f32[64,128,128]{1,2,0:T(8,128)} %get-tuple-element.359, f32[64,64,128]{2,1,0:T(8,128)S(1)} %fusion.189, bf16[64,64,128]{2,1,0:T(8,128)(2,1)S(1)} %fusion.190, pred[]{:T(512)S(6)} %compare.16, f32[64,128]{1,0:T(8,128)S(1)} %get-tuple-element.314, ...), kind=kOutput, calls=%fused_computation.24.clone.1 | convolution fusion | flops 808976384 | bytes 11599877 | tf_op jit(solution)/shard_map/while/body/eval_jaxpr/gb,dgi->dbi/dot_general | solution.py:106
  668.0 5.4 copy.15
  673.5 5.6 copy.14
  679.1 6.9 copy.62
  688.4 61.7 %reduce-scatter.3.cloned.1.call-done = f32[64,32,128]{2,0,1:T(8,128)} async-done(((f32[64,128,128]{2,0,1:T(8,128)}), f32[64,32,128]{2,0,1:T(8,128)}) %reduce-scatter.3.cloned.1.call-update) | async-done | bytes 1048592 | tf_op jit(solution)/shard_map/reduce_scatter | solution.py:121
  755.3 79.5 %all-reduce.4.cloned.1.call-done = f32[64,16384]{1,0:T(8,128)} async-done(((f32[64,16384]{1,0:T(8,128)}), f32[64,16384]{1,0:T(8,128)}) %all-reduce.4.cloned.1.call-update) | async-done | bytes 4194320 | tf_op jit(solution)/shard_map/psum | solution.py:119
  834.8 139.9 %reduce-scatter.5.cloned.1.call-done = f32[1,64,64]{2,1,0:T(8,128)} async-done(((f32[32,64,64]{2,1,0:T(8,128)}), f32[1,64,64]{2,1,0:T(8,128)}) %reduce-scatter.5.cloned.1.call-update) | async-done | bytes 16400 | tf_op jit(solution)/shard_map/reduce_scatter | solution.py:132
  974.7 4.5 copy.95
  (186 shorter events, 103.7 us)
Async XLA Ops:
  7.2 285.2 %all-reduce.6.cloned.1.call-start = ((), (), s32[]{:S(2)}) async-start(), calls=%async_computation.5 | async-start | bytes 262144 | tf_op jit(solution)/shard_map/psum | solution.py:78
  9.2 4.4 copy-start.3
  17.6 84.6 %copy-start.8 = (s32[1,1,512]{2,1,0:T(1,128)S(1)}, s32[1,1,512]{2,1,0:T(1,128)}, u32[]{:S(2)}) copy-start(s32[1,1,512]{2,1,0:T(1,128)} %param.17) | copy-start | bytes 6148
  17.6 1.6 copy-start
  28.2 1.6 copy-start
  38.8 1.6 copy-start
  49.3 1.6 copy-start
  59.9 1.6 copy-start
  70.4 1.6 copy-start
  81.0 1.6 copy-start
  91.6 1.6 copy-start
  135.0 1.5 collective-permute-start
  136.4 58.8 %collective-permute-start.1 = (f32[16384]{0:T(1024)S(1)}, f32[16384]{0:T(1024)S(1)}, u32[]{:S(2)}, u32[]{:S(2)}) collective-permute-start(f32[16384]{0:T(1024)S(1)} %add.79), channel_id=1, source_target_pairs={{0,8},{4,12},{8,0},{12,4},{16,24},{20,28},{24,16},{28,20},{1,9},{5... | collective-permute-start | bytes 196616 | tf_op jit(solution)/shard_map/ppermute | solution.py:81
  139.3 60.2 %copy-start.4 = (f32[16384]{0:T(1024)S(1)}, f32[16384]{0:T(1024)}, u32[]{:S(2)}) copy-start(f32[16384]{0:T(1024)} %param.16) | copy-start | bytes 196612
  195.2 4.3 collective-permute-start.2
  199.9 92.5 %copy-start.5 = (f32[16384]{0:T(1024)S(1)}, f32[16384]{0:T(1024)}, u32[]{:S(2)}) copy-start(f32[16384]{0:T(1024)} %param.15) | copy-start | bytes 196612
  257.2 493.0 %reduce-scatter.3.cloned.1.call-start = ((), (), s32[]{:S(2)}) async-start(), calls=%async_computation.3 | async-start | bytes 5242880 | tf_op jit(solution)/shard_map/reduce_scatter | solution.py:121
  293.5 39.9 %copy-start.6 = (f32[16384]{0:T(1024)S(1)}, f32[16384]{0:T(1024)}, u32[]{:S(2)}) copy-start(f32[16384]{0:T(1024)} %get-tuple-element.185) | copy-start | bytes 196612
  293.5 39.8 %copy-start.7 = (f32[16384]{0:T(1024)S(1)}, f32[16384]{0:T(1024)}, u32[]{:S(2)}) copy-start(f32[16384]{0:T(1024)} %get-tuple-element.184) | copy-start | bytes 196612
  326.2 1.3 collective-permute-start.3
  327.5 4.3 collective-permute-start.4
  331.9 4.3 collective-permute-start.5
  339.7 9.7 copy-start.1
  351.6 10.6 %copy-start.2 = (bf16[64,64,128]{2,1,0:T(8,128)(2,1)S(1)}, bf16[64,64,128]{2,1,0:T(8,128)(2,1)}, u32[]{:S(2)}) copy-start(bf16[64,64,128]{2,1,0:T(8,128)(2,1)} %fusion.186) | copy-start | bytes 3145732 | tf_op jit(solution)/shard_map/while
  379.1 9.7 copy-start.1
  391.0 11.2 %copy-start.2 = (bf16[64,64,128]{2,1,0:T(8,128)(2,1)S(1)}, bf16[64,64,128]{2,1,0:T(8,128)(2,1)}, u32[]{:S(2)}) copy-start(bf16[64,64,128]{2,1,0:T(8,128)(2,1)} %fusion.186) | copy-start | bytes 3145732 | tf_op jit(solution)/shard_map/while
  420.7 9.7 copy-start.1
  432.6 11.2 %copy-start.2 = (bf16[64,64,128]{2,1,0:T(8,128)(2,1)S(1)}, bf16[64,64,128]{2,1,0:T(8,128)(2,1)}, u32[]{:S(2)}) copy-start(bf16[64,64,128]{2,1,0:T(8,128)(2,1)} %fusion.186) | copy-start | bytes 3145732 | tf_op jit(solution)/shard_map/while
  462.3 9.7 copy-start.1
  474.2 11.2 %copy-start.2 = (bf16[64,64,128]{2,1,0:T(8,128)(2,1)S(1)}, bf16[64,64,128]{2,1,0:T(8,128)(2,1)}, u32[]{:S(2)}) copy-start(bf16[64,64,128]{2,1,0:T(8,128)(2,1)} %fusion.186) | copy-start | bytes 3145732 | tf_op jit(solution)/shard_map/while
  503.9 9.7 copy-start.1
  515.8 11.2 %copy-start.2 = (bf16[64,64,128]{2,1,0:T(8,128)(2,1)S(1)}, bf16[64,64,128]{2,1,0:T(8,128)(2,1)}, u32[]{:S(2)}) copy-start(bf16[64,64,128]{2,1,0:T(8,128)(2,1)} %fusion.186) | copy-start | bytes 3145732 | tf_op jit(solution)/shard_map/while
  545.5 9.7 copy-start.1
  557.4 11.2 %copy-start.2 = (bf16[64,64,128]{2,1,0:T(8,128)(2,1)S(1)}, bf16[64,64,128]{2,1,0:T(8,128)(2,1)}, u32[]{:S(2)}) copy-start(bf16[64,64,128]{2,1,0:T(8,128)(2,1)} %fusion.186) | copy-start | bytes 3145732 | tf_op jit(solution)/shard_map/while
  587.1 9.7 copy-start.1
  599.0 11.2 %copy-start.2 = (bf16[64,64,128]{2,1,0:T(8,128)(2,1)S(1)}, bf16[64,64,128]{2,1,0:T(8,128)(2,1)}, u32[]{:S(2)}) copy-start(bf16[64,64,128]{2,1,0:T(8,128)(2,1)} %fusion.186) | copy-start | bytes 3145732 | tf_op jit(solution)/shard_map/while
  628.7 9.7 copy-start.1
  640.6 11.2 %copy-start.2 = (bf16[64,64,128]{2,1,0:T(8,128)(2,1)S(1)}, bf16[64,64,128]{2,1,0:T(8,128)(2,1)}, u32[]{:S(2)}) copy-start(bf16[64,64,128]{2,1,0:T(8,128)(2,1)} %fusion.186) | copy-start | bytes 3145732 | tf_op jit(solution)/shard_map/while
  673.5 161.3 %all-reduce.4.cloned.1.call-start = ((), (), s32[]{:S(2)}) async-start(), calls=%async_computation.2 | async-start | bytes 8388608 | tf_op jit(solution)/shard_map/psum | solution.py:119
  686.0 2.3 copy-start.9
  686.1 288.7 %reduce-scatter.5.cloned.1.call-start = ((), (), s32[]{:S(2)}) async-start(), calls=%async_computation.4 | async-start | bytes 1081344 | tf_op jit(solution)/shard_map/reduce_scatter | solution.py:132
Sparse Core Ops, SparseCore 0:
  257.3 35.0 all-reduce.5
  673.6 76.5 reduce-scatter.2
  753.4 81.3 all-reduce.3
  837.5 137.2 reduce-scatter.4
